TPU v7x, 32 devices: a whole 2x2x4 slice. The times are simulated.
32 devices in a mesh: seq: 16 (over z, x, core), head: 2 (over y).
Axes of the slice: x: 2, y: 2, z: 4, core: 2. Of those that a mesh axis runs over, the one named last changes fastest.
Arguments:
- queries: bfloat16 [8192, 3072], P(('seq', 'head'))
- keys: bfloat16 [8192, 3072], P(('seq', 'head'))
- values: bfloat16 [8192, 3072], P(('seq', 'head')), may hold values from -6 to 6
- kv_blocks: int32 [64, 64], replicated, may hold values from 0 to 63, as said below
- block_counts: int32 [64, 16], replicated, may hold values from 0 to 4, as said below
Outputs:
- attended: bfloat16 [8192, 3072], P(('seq', 'head'))
Inputs may be any that keep to these rules, and one draw needn't show every extreme that they name: `kv_blocks`: slot f * 4 + j names a key block of frame f, as a global block index f * 4 + local; the valid slots of one query block and frame name distinct blocks; slots at or beyond block_counts carry a block of the same frame and no meaning. With e the distance between frame f and the frame of query block b: block_counts[b, f] is 4 where e is 0, at most 2 where e is 1, at most 1 where e is 2, 3 or a power of two, and 0 otherwise; each of these largest values is taken by the first query block of every frame.
All inputs are finite; a program needn't handle non-finite values.
Results may differ from a plain program's by a relative error of at most 0.02.
Values may be sent and summed in bfloat16 or wider, within the bound.
A program may use at most 128 MiB of HBM per device.

v0:
```python
import jax
import jax.numpy as jnp
from jax import lax
from jax.sharding import PartitionSpec as P

HD = 128
BLK = 128
SLOTS = 4
NEG_FILL = -1e30


def from_behind(block, axis, distance):
    devices = range(lax.axis_size(axis))
    route = [(i - distance, i) for i in devices if i - distance in devices]
    return lax.ppermute(block, axis, route)


def rotate_time(matrix, frame_ids):
    row_count = matrix.shape[0]
    head_count = matrix.shape[1] // HD
    per_head = matrix.reshape(row_count, head_count, HD)
    pair_index = jnp.arange(8, dtype=jnp.float32)
    frequency = 256.0 ** (-pair_index / 8.0)
    angles = frame_ids.astype(jnp.float32)[:, None] * frequency[None, :]
    cosine = jnp.cos(angles)[:, None, :]
    sine_part = jnp.sin(angles)[:, None, :]
    pair_view = per_head[:, :, :16].reshape(row_count, head_count, 8, 2)
    even_part = pair_view[..., 0]
    odd_part = pair_view[..., 1]
    turned = jnp.stack(
        [even_part * cosine - odd_part * sine_part, even_part * sine_part + odd_part * cosine],
        axis=-1,
    )
    joined = jnp.concatenate(
        [turned.reshape(row_count, head_count, 16), per_head[:, :, 16:]], axis=2
    )
    return joined.reshape(row_count, head_count * HD)


def signed_distances(frame_count):
    base = [1, 2, 3]
    power = 4
    while power < frame_count:
        base.append(power)
        power = power * 2
    result = [0]
    for step in base:
        result.append(step)
        result.append(-step)
    return result


def slot_cap(distance):
    if distance == 0:
        return SLOTS
    if abs(distance) == 1:
        return 2
    return 1


def block_table(kv_blocks, block_counts, query_frame, key_frame, cap, frame_blocks, frame_count):
    valid = (
        (query_frame >= 0)
        & (query_frame < frame_count)
        & (key_frame >= 0)
        & (key_frame < frame_count)
    )
    query_clip = jnp.clip(query_frame, 0, frame_count - 1)
    key_clip = jnp.clip(key_frame, 0, frame_count - 1)
    row_start = query_clip * frame_blocks
    block_ids = (
        lax.dynamic_slice(kv_blocks, (row_start, key_clip * SLOTS), (frame_blocks, cap))
        - key_clip * frame_blocks
    )
    counts = lax.dynamic_slice(block_counts, (row_start, key_clip), (frame_blocks, 1))[:, 0]
    return (block_ids, jnp.where(valid, counts, 0), valid)


def frame_partial(query_group, key_blocks, value_blocks, block_ids, valid_counts, cap):
    picked_keys = key_blocks[block_ids]
    picked_values = value_blocks[block_ids]
    scores = jnp.einsum(
        "bqhd,bskhd->bhqsk", query_group, picked_keys, preferred_element_type=jnp.float32
    ) * HD ** (-0.5)
    usable = (jnp.arange(cap, dtype=jnp.int32)[None, :] < valid_counts[:, None])[
        :, None, None, :, None
    ]
    masked = jnp.where(usable, scores, NEG_FILL)
    part_max = jnp.max(masked, axis=(3, 4))
    probs = jnp.where(usable, jnp.exp(masked - part_max[..., None, None]), 0.0)
    part_sum = jnp.sum(probs, axis=(3, 4))
    part_num = jnp.einsum(
        "bhqsk,bskhd->bqhd",
        probs.astype(jnp.bfloat16),
        picked_values,
        preferred_element_type=jnp.float32,
    )
    return (part_num.astype(jnp.bfloat16), part_max, part_sum)


def guarded_partial(query_group, key_blocks, value_blocks, block_ids, valid_counts, cap):
    return frame_partial(query_group, key_blocks, value_blocks, block_ids, valid_counts, cap)


def merge_state(state, part):
    run_max, run_sum, run_num = state
    part_num, part_max, part_sum = part
    new_max = jnp.maximum(run_max, part_max)
    old_scale = jnp.exp(run_max - new_max)
    new_scale = jnp.exp(part_max - new_max)
    run_sum = old_scale * run_sum + new_scale * part_sum
    run_num = (
        run_num * jnp.transpose(old_scale, (0, 2, 1))[..., None]
        + part_num.astype(jnp.float32) * jnp.transpose(new_scale, (0, 2, 1))[..., None]
    )
    return (new_max, run_sum, run_num)


def local(queries, keys, values, kv_blocks, block_counts):
    seq_index = lax.axis_index("seq")
    frame_count = lax.axis_size("seq")
    query_slab = lax.all_to_all(queries, "head", split_axis=1, concat_axis=0, tiled=True)
    key_slab, value_slab = (
        lax.all_to_all(keys, "head", split_axis=1, concat_axis=0, tiled=True),
        lax.all_to_all(values, "head", split_axis=1, concat_axis=0, tiled=True),
    )
    frame_tokens = key_slab.shape[0]
    row_width = key_slab.shape[1]
    head_count = row_width // HD
    frame_blocks = frame_tokens // BLK
    frame_ids = jnp.zeros((frame_tokens,), jnp.int32) + seq_index
    query_turned = rotate_time(query_slab.astype(jnp.float32), frame_ids).astype(jnp.bfloat16)
    key_turned = rotate_time(key_slab.astype(jnp.float32), frame_ids).astype(jnp.bfloat16)
    query_group = query_turned.reshape(frame_blocks, BLK, head_count, HD)
    key_blocks = key_turned.reshape(frame_blocks, BLK, head_count, HD)
    value_blocks = value_slab.reshape(frame_blocks, BLK, head_count, HD)
    stat_shape = (frame_blocks, head_count, BLK)
    state = (
        jnp.full(stat_shape, NEG_FILL, jnp.float32),
        jnp.zeros(stat_shape, jnp.float32),
        jnp.zeros((frame_blocks, BLK, head_count, HD), jnp.float32),
    )
    for distance in signed_distances(frame_count):
        cap = slot_cap(distance)
        if distance == 0:
            block_ids, counts, valid = block_table(
                kv_blocks, block_counts, seq_index, seq_index, cap, frame_blocks, frame_count
            )
            part = frame_partial(query_group, key_blocks, value_blocks, block_ids, counts, cap)
        else:
            far_keys, far_values = from_behind((key_blocks, value_blocks), "seq", distance)
            block_ids, counts, valid = block_table(
                kv_blocks,
                block_counts,
                seq_index,
                seq_index - distance,
                cap,
                frame_blocks,
                frame_count,
            )
            part = guarded_partial(query_group, far_keys, far_values, block_ids, counts, cap)
        state = merge_state(state, part)
    denominator = jnp.transpose(state[1], (0, 2, 1))[..., None]
    attended = (state[2] / denominator).reshape(frame_tokens, row_width).astype(jnp.bfloat16)
    return lax.all_to_all(attended, "head", split_axis=0, concat_axis=1, tiled=True)


def solution(mesh):
    in_specs = (
        P(("seq", "head"), None),
        P(("seq", "head"), None),
        P(("seq", "head"), None),
        P(),
        P(),
    )
    out_specs = P(("seq", "head"), None)
    return jax.shard_map(local, mesh=mesh, in_specs=in_specs, out_specs=out_specs, check_vma=False)
```

profile of v0, /device:TPU:26, one launch (start us, length us, event | category | flops | bytes accessed | tf_op | source)
XLA Modules:
  0.0 654.6 jit_solution(9133775101212698396)
XLA Ops:
  2.7 3.7 all-to-all-start.1
  9.5 16.3 %all-to-all-done.1 = bf16[256,2,1536]{0,2,1:T(8,128)(2,1)S(1)} async-done(((bf16[256,2,1536]{0,2,1:T(8,128)(2,1)}), bf16[256,2,1536]{0,2,1:T(8,128)(2,1)S(1)}, u32[]{:S(2)}, u32[]{:S(2)}) %all-to-all-start.1) | async-done | bytes 1572896 | tf_op jit(solution)/shard_map/all_to_all | solution.py:124
  25.9 3.7 all-to-all-start.2
  35.6 12.6 %all-to-all-done.2 = bf16[256,2,1536]{0,2,1:T(8,128)(2,1)S(1)} async-done(((bf16[256,2,1536]{0,2,1:T(8,128)(2,1)}), bf16[256,2,1536]{0,2,1:T(8,128)(2,1)S(1)}, u32[]{:S(2)}, u32[]{:S(2)}) %all-to-all-start.2) | async-done | bytes 1572896 | tf_op jit(solution)/shard_map/all_to_all | solution.py:125
  48.1 4.6 all-to-all-start
  54.6 10.7 %copy.203 = bf16[2,256,1536]{1,0,2:T(2,128)(2,1)} copy(bf16[2,256,1536]{1,2,0:T(8,128)(2,1)S(1)} %bitcast.448) | data formatting | bytes 3145728 | tf_op jit(solution)/shard_map/all_to_all | solution.py:125
  65.3 5.2 reshape.374
  79.4 10.7 %copy.195 = bf16[2,256,1536]{1,0,2:T(2,128)(2,1)} copy(bf16[2,256,1536]{1,2,0:T(8,128)(2,1)S(1)} %bitcast.447) | data formatting | bytes 3145728 | tf_op jit(solution)/shard_map/convert_element_type | solution.py:133
  94.1 4.8 copy.188
  106.9 3.7 concatenate.22
  115.3 3.7 copy.200
  120.5 4.0 pad_maximum_fusion.1
  125.8 6.1 collective-permute-start.10
  136.0 4.0 gather_fusion.1
  140.0 5.5 gather_fusion
  146.7 3.7 copy.193
  152.2 4.3 copy.201
  157.4 5.6 fusion
  163.1 5.7 collective-permute-start.7
  170.1 9.9 %collective-permute-done.12 = bf16[4,128,12,128]{3,1,2,0:T(8,128)(2,1)} collective-permute-done((bf16[4,128,12,128]{3,1,2,0:T(8,128)(2,1)}, bf16[4,128,12,128]{3,1,2,0:T(8,128)(2,1)}, u32[]{:S(2)}, u32[]{:S(2)}) %collective-permute-start.12) | collective-permute-done | bytes 1572896 | tf_op jit(solution)/shard_map/ppermute | solution.py:15
  183.7 11.9 %bitcast_convert_fusion.2 = bf16[4,12,128,128]{3,2,1,0:T(8,128)(2,1)} fusion(f32[4,12,128,512]{2,3,1,0} %get-tuple-element.88, f32[4,12,128]{2,1,0:T(8,128)S(1)} %get-tuple-element.87, pred[4,4]{1,0:T(4,128)(4,1)S(1)} %copy-done.73, bf16[4,4,128,12,128]{4,2,3,1,0:T(8,128)(2,1)} %bitcast.446), kind=kOutput, calls=%fused_computation.84 | convolution fusion | flops 821821440 | bytes 20471824 | tf_op jit(solution)/shard_map/bhqsk,bskhd->bqhd/dot_general | solution.py:92
  195.5 12.2 %collective-permute-done.8 = bf16[4,128,12,128]{3,1,2,0:T(8,128)(2,1)} collective-permute-done((bf16[4,128,12,128]{3,1,2,0:T(8,128)(2,1)}, bf16[4,128,12,128]{3,1,2,0:T(8,128)(2,1)}, u32[]{:S(2)}, u32[]{:S(2)}) %collective-permute-start.8) | collective-permute-done | bytes 1572896 | tf_op jit(solution)/shard_map/ppermute | solution.py:15
  209.2 6.6 %fusion.1 = f32[4,12,128]{2,1,0:T(8,128)S(1)} fusion(f32[4,12,128,512]{2,3,1,0} %get-tuple-element.88, f32[4,12,128]{2,1,0:T(8,128)S(1)} %get-tuple-element.87, pred[4,4]{1,0:T(4,128)(4,1)S(1)} %copy-done.73), kind=kLoop, calls=%fused_computation.25 | loop fusion | flops 15722496 | bytes 12632080 | tf_op jit(solution)/shard_map/reduce_sum | solution.py:91
  222.6 3.5 gather_fusion.13
  236.3 48.8 %collective-permute-done.7 = bf16[4,128,12,128]{3,1,2,0:T(8,128)(2,1)} collective-permute-done((bf16[4,128,12,128]{3,1,2,0:T(8,128)(2,1)S(1)}, bf16[4,128,12,128]{3,1,2,0:T(8,128)(2,1)}, u32[]{:S(2)}, u32[]{:S(2)}) %collective-permute-start.7) | collective-permute-done | bytes 1572896 | tf_op jit(solution)/shard_map/ppermute | solution.py:15
  285.2 9.1 %collective-permute-start.19 = (bf16[4,128,12,128]{3,1,2,0:T(8,128)(2,1)S(1)}, bf16[4,128,12,128]{3,1,2,0:T(8,128)(2,1)}, u32[]{:S(2)}, u32[]{:S(2)}) collective-permute-start(bf16[4,128,12,128]{3,1,2,0:T(8,128)(2,1)S(1)} %copy.204), channel_id=1, source_target_pairs={{16,0},{18,2},{20,4},{22,6},{24,8},{26,10},{28,12},{30,14},{17,1},... | collective-permute-start | bytes 4718600 | tf_op jit(solution)/shard_map/ppermute | solution.py:15
  297.6 21.3 %collective-permute-done.6 = bf16[4,128,12,128]{3,1,2,0:T(8,128)(2,1)} collective-permute-done((bf16[4,128,12,128]{3,1,2,0:T(8,128)(2,1)}, bf16[4,128,12,128]{3,1,2,0:T(8,128)(2,1)}, u32[]{:S(2)}, u32[]{:S(2)}) %collective-permute-start.6) | collective-permute-done | bytes 1572896 | tf_op jit(solution)/shard_map/ppermute | solution.py:15
  319.0 7.5 %collective-permute-start.15 = (bf16[4,128,12,128]{3,1,2,0:T(8,128)(2,1)S(1)}, bf16[4,128,12,128]{3,1,2,0:T(8,128)(2,1)}, u32[]{:S(2)}, u32[]{:S(2)}) collective-permute-start(bf16[4,128,12,128]{3,1,2,0:T(8,128)(2,1)S(1)} %copy.204), channel_id=1, source_target_pairs={{8,0},{10,2},{12,4},{14,6},{16,8},{18,10},{20,12},{22,14},{24,16},... | collective-permute-start | bytes 4718600 | tf_op jit(solution)/shard_map/ppermute | solution.py:15
  338.3 3.5 gather_fusion.6
  341.7 4.4 fusion.56
  361.0 4.4 fusion.60
  373.5 52.1 %collective-permute-done.14 = bf16[4,128,12,128]{3,1,2,0:T(8,128)(2,1)} collective-permute-done((bf16[4,128,12,128]{3,1,2,0:T(8,128)(2,1)}, bf16[4,128,12,128]{3,1,2,0:T(8,128)(2,1)}, u32[]{:S(2)}, u32[]{:S(2)}) %collective-permute-start.14) | collective-permute-done | bytes 1572896 | tf_op jit(solution)/shard_map/ppermute | solution.py:15
  431.4 4.4 fusion.61
  445.2 4.0 gather_fusion.4
  449.2 4.0 copy.211
  453.2 3.6 collective-permute-start.3
  456.9 4.0 gather_fusion.2
  463.2 3.7 fusion.11
  466.9 3.7 fusion.12
  476.0 5.2 fusion.13
  489.0 4.3 convolution_convert_fusion.2
  498.9 82.6 %collective-permute-done.17 = bf16[4,128,12,128]{3,1,2,0:T(8,128)(2,1)} collective-permute-done((bf16[4,128,12,128]{3,1,2,0:T(8,128)(2,1)S(1)}, bf16[4,128,12,128]{3,1,2,0:T(8,128)(2,1)}, u32[]{:S(2)}, u32[]{:S(2)}) %collective-permute-start.17) | collective-permute-done | bytes 1572896 | tf_op jit(solution)/shard_map/ppermute | solution.py:15
  584.0 4.3 convolution_convert_fusion.1
  595.3 4.0 gather_fusion.5
  599.3 4.1 gather_fusion.3
  603.4 7.2 %bitcast_convert_fusion.1 = bf16[4,12,128,128]{3,2,1,0:T(8,128)(2,1)} fusion(f32[4,12,128,256]{2,3,1,0} %get-tuple-element.86, f32[4,12,128]{2,1,0:T(8,128)S(1)} %get-tuple-element.85, pred[4,2]{1,0:T(4,128)(4,1)S(1)} %copy-done.54, bf16[4,2,128,12,128]{4,2,3,1,0:T(8,128)(2,1)} %bitcast.453), kind=kOutput, calls=%fused_computation.79 | convolution fusion | flops 411303936 | bytes 11034632 | tf_op jit(solution)/shard_map/bhqsk,bskhd->bqhd/dot_general | solution.py:92
  617.6 9.7 %fusion.23 = bf16[4,128,12,128]{1,3,2,0:T(8,128)(2,1)S(1)} fusion(bf16[4,12,128,128]{3,2,1,0:T(8,128)(2,1)} %convolution_convert_fusion.1, bf16[4,12,128,128]{3,2,1,0:T(8,128)(2,1)} %convolution_convert_fusion.2, bf16[4,12,128,128]{3,2,1,0:T(8,128)(2,1)} %convolution_convert_fusion.3, bf16[4,12,128,128]{3,2,1,0:T(8,128)(2,1)} %convolution_convert_fusion.4, ...), kind=kOutput, calls=%fused_computation.49 | convolution fusion | flops 241434624 | bytes 22609924 | tf_op jit(solution)/shard_map/bhqsk,bskhd->bqhd/dot_general | solution.py:92
  629.9 22.8 %all_to_all.58 = bf16[2,256,1536]{1,2,0:T(8,128)(2,1)S(1)} all-to-all(bf16[2,256,1536]{1,2,0:T(8,128)(2,1)S(1)} %copy.248), channel_id=1, replica_groups=mesh['seq'=16,'head'=2] {'head'}, dimensions={0} | all-to-all | bytes 3145728 | tf_op jit(solution)/shard_map/all_to_all | solution.py:165
  (284 shorter events, 168.1 us)
Async XLA Ops:
  0.0 6.4 copy-start.51
  0.0 7.4 %copy-start.31 = (bf16[256,3072]{1,0:T(8,128)(2,1)S(1)}, bf16[256,3072]{1,0:T(8,128)(2,1)}, u32[]{:S(2)}) copy-start(bf16[256,3072]{1,0:T(8,128)(2,1)} %param.7) | copy-start | bytes 4718596
  2.7 23.2 %all-to-all-start.1 = ((bf16[256,2,1536]{0,2,1:T(8,128)(2,1)}), bf16[256,2,1536]{0,2,1:T(8,128)(2,1)S(1)}, u32[]{:S(2)}, u32[]{:S(2)}) async-start(bf16[256,2,1536]{0,2,1:T(8,128)(2,1)} %bitcast.3), calls=%async_computation.1 | async-start | bytes 3145728 | tf_op jit(solution)/shard_map/all_to_all | solution.py:124
  25.9 22.3 %all-to-all-start.2 = ((bf16[256,2,1536]{0,2,1:T(8,128)(2,1)}), bf16[256,2,1536]{0,2,1:T(8,128)(2,1)S(1)}, u32[]{:S(2)}, u32[]{:S(2)}) async-start(bf16[256,2,1536]{0,2,1:T(8,128)(2,1)} %bitcast.449), calls=%async_computation.2 | async-start | bytes 3145728 | tf_op jit(solution)/shard_map/all_to_all | solution.py:125
  48.1 46.0 %all-to-all-start = ((bf16[256,2,1536]{0,2,1:T(8,128)(2,1)}), bf16[256,2,1536]{0,2,1:T(8,128)(2,1)}, u32[]{:S(2)}, u32[]{:S(2)}) async-start(bf16[256,2,1536]{0,2,1:T(8,128)(2,1)} %bitcast.450), calls=%async_computation | async-start | bytes 3145728 | tf_op jit(solution)/shard_map/all_to_all | solution.py:122
  73.2 61.3 %collective-permute-start.13 = (bf16[4,128,12,128]{3,1,2,0:T(8,128)(2,1)S(1)}, bf16[4,128,12,128]{3,1,2,0:T(8,128)(2,1)}, u32[]{:S(2)}, u32[]{:S(2)}) collective-permute-start(bf16[4,128,12,128]{3,1,2,0:T(8,128)(2,1)S(1)} %copy.204), channel_id=1, source_target_pairs={{0,8},{2,10},{4,12},{6,14},{8,16},{10,18},{12,20},{14,22},{16,24},... | collective-permute-start | bytes 4718600 | tf_op jit(solution)/shard_map/ppermute | solution.py:15
  74.5 88.6 %collective-permute-start.11 = (bf16[4,128,12,128]{3,1,2,0:T(8,128)(2,1)S(1)}, bf16[4,128,12,128]{3,1,2,0:T(8,128)(2,1)}, u32[]{:S(2)}, u32[]{:S(2)}) collective-permute-start(bf16[4,128,12,128]{3,1,2,0:T(8,128)(2,1)S(1)} %copy.204), channel_id=1, source_target_pairs={{6,0},{8,2},{10,4},{12,6},{14,8},{16,10},{18,12},{20,14},{22,16},{... | collective-permute-start | bytes 4718600 | tf_op jit(solution)/shard_map/ppermute | solution.py:15
  77.6 91.2 %collective-permute-start.9 = (bf16[4,128,12,128]{3,1,2,0:T(8,128)(2,1)S(1)}, bf16[4,128,12,128]{3,1,2,0:T(8,128)(2,1)}, u32[]{:S(2)}, u32[]{:S(2)}) collective-permute-start(bf16[4,128,12,128]{3,1,2,0:T(8,128)(2,1)S(1)} %copy.204), channel_id=1, source_target_pairs={{0,6},{2,8},{4,10},{6,12},{8,14},{10,16},{12,18},{14,20},{16,22},{... | collective-permute-start | bytes 4718600 | tf_op jit(solution)/shard_map/ppermute | solution.py:15
  101.8 34.2 %copy-start.22 = (bf16[512,12,128]{0,2,1:T(8,128)(2,1)}, bf16[512,12,128]{0,2,1:T(8,128)(2,1)S(1)}, u32[]{:S(2)}) copy-start(bf16[512,12,128]{0,2,1:T(8,128)(2,1)S(1)} %convert_element_type.184) | copy-start | bytes 4718596
  119.0 13.6 %copy-start.74 = (s32[4,1]{0,1:T(1,128)S(1)}, s32[4,1]{0,1:T(1,128)}, u32[]{:S(2)}) copy-start(s32[4,1]{0,1:T(1,128)} %copy.289) | copy-start | bytes 52
  119.0 17.0 %copy-start.32 = (bf16[512,12,8,1]{0,2,3,1:T(8,128)(2,1)S(1)}, bf16[512,12,8,1]{0,2,3,1:T(8,128)(2,1)}, u32[]{:S(2)}) copy-start(bf16[512,12,8,1]{0,2,3,1:T(8,128)(2,1)} %get-tuple-element.67) | copy-start | bytes 294916
  119.0 17.0 %copy-start.33 = (bf16[512,12,8,1]{0,2,3,1:T(8,128)(2,1)S(1)}, bf16[512,12,8,1]{0,2,3,1:T(8,128)(2,1)}, u32[]{:S(2)}) copy-start(bf16[512,12,8,1]{0,2,3,1:T(8,128)(2,1)} %get-tuple-element.68) | copy-start | bytes 294916
  120.5 11.4 %copy-start.72 = (s32[64,16]{0,1:T(8,128)S(1)}, s32[64,16]{0,1:T(8,128)}, u32[]{:S(2)}) copy-start(s32[64,16]{0,1:T(8,128)} %param.9) | copy-start | bytes 12292
  120.5 11.4 %copy-start.75 = (s32[4,1]{0,1:T(1,128)S(1)}, s32[4,1]{0,1:T(1,128)}, u32[]{:S(2)}) copy-start(s32[4,1]{0,1:T(1,128)} %copy.288) | copy-start | bytes 52
  124.5 55.5 %collective-permute-start.12 = (bf16[4,128,12,128]{3,1,2,0:T(8,128)(2,1)}, bf16[4,128,12,128]{3,1,2,0:T(8,128)(2,1)}, u32[]{:S(2)}, u32[]{:S(2)}) collective-permute-start(bf16[4,128,12,128]{3,1,2,0:T(8,128)(2,1)} %pad_maximum_fusion.1), channel_id=1, source_target_pairs={{0,8},{2,10},{4,12},{6,14},{8,16},{10,18},{12,20},{14,22},{16,24},... | collective-permute-start | bytes 4718600 | tf_op jit(solution)/shard_map/ppermute | solution.py:15
  125.8 56.6 %collective-permute-start.10 = (bf16[4,128,12,128]{3,1,2,0:T(8,128)(2,1)}, bf16[4,128,12,128]{3,1,2,0:T(8,128)(2,1)}, u32[]{:S(2)}, u32[]{:S(2)}) collective-permute-start(bf16[4,128,12,128]{3,1,2,0:T(8,128)(2,1)} %pad_maximum_fusion.1), channel_id=1, source_target_pairs={{6,0},{8,2},{10,4},{12,6},{14,8},{16,10},{18,12},{20,14},{22,16},{... | collective-permute-start | bytes 4718600 | tf_op jit(solution)/shard_map/ppermute | solution.py:15
  134.5 73.2 %collective-permute-start.8 = (bf16[4,128,12,128]{3,1,2,0:T(8,128)(2,1)}, bf16[4,128,12,128]{3,1,2,0:T(8,128)(2,1)}, u32[]{:S(2)}, u32[]{:S(2)}) collective-permute-start(bf16[4,128,12,128]{3,1,2,0:T(8,128)(2,1)} %pad_maximum_fusion.1), channel_id=1, source_target_pairs={{0,6},{2,8},{4,10},{6,12},{8,14},{10,16},{12,18},{14,20},{16,22},{... | collective-permute-start | bytes 4718600 | tf_op jit(solution)/shard_map/ppermute | solution.py:15
  140.0 5.5 slice-start
  163.1 122.1 %collective-permute-start.7 = (bf16[4,128,12,128]{3,1,2,0:T(8,128)(2,1)S(1)}, bf16[4,128,12,128]{3,1,2,0:T(8,128)(2,1)}, u32[]{:S(2)}, u32[]{:S(2)}) collective-permute-start(bf16[4,128,12,128]{3,1,2,0:T(8,128)(2,1)S(1)} %copy.204), channel_id=1, source_target_pairs={{4,0},{6,2},{8,4},{10,6},{12,8},{14,10},{16,12},{18,14},{20,16},{2... | collective-permute-start | bytes 4718600 | tf_op jit(solution)/shard_map/ppermute | solution.py:15
  168.8 161.1 %collective-permute-start.5 = (bf16[4,128,12,128]{3,1,2,0:T(8,128)(2,1)S(1)}, bf16[4,128,12,128]{3,1,2,0:T(8,128)(2,1)}, u32[]{:S(2)}, u32[]{:S(2)}) collective-permute-start(bf16[4,128,12,128]{3,1,2,0:T(8,128)(2,1)S(1)} %copy.204), channel_id=1, source_target_pairs={{0,4},{2,6},{4,8},{6,10},{8,12},{10,14},{12,16},{14,18},{16,20},{1... | collective-permute-start | bytes 4718600 | tf_op jit(solution)/shard_map/ppermute | solution.py:15
  180.0 139.0 %collective-permute-start.6 = (bf16[4,128,12,128]{3,1,2,0:T(8,128)(2,1)}, bf16[4,128,12,128]{3,1,2,0:T(8,128)(2,1)}, u32[]{:S(2)}, u32[]{:S(2)}) collective-permute-start(bf16[4,128,12,128]{3,1,2,0:T(8,128)(2,1)} %pad_maximum_fusion.1), channel_id=1, source_target_pairs={{4,0},{6,2},{8,4},{10,6},{12,8},{14,10},{16,12},{18,14},{20,16},{2... | collective-permute-start | bytes 4718600 | tf_op jit(solution)/shard_map/ppermute | solution.py:15
  182.4 153.4 %collective-permute-start.4 = (bf16[4,128,12,128]{3,1,2,0:T(8,128)(2,1)}, bf16[4,128,12,128]{3,1,2,0:T(8,128)(2,1)}, u32[]{:S(2)}, u32[]{:S(2)}) collective-permute-start(bf16[4,128,12,128]{3,1,2,0:T(8,128)(2,1)} %pad_maximum_fusion.1), channel_id=1, source_target_pairs={{0,4},{2,6},{4,8},{6,10},{8,12},{10,14},{12,16},{14,18},{16,20},{1... | collective-permute-start | bytes 4718600 | tf_op jit(solution)/shard_map/ppermute | solution.py:15
  207.7 147.3 %collective-permute-start.16 = (bf16[4,128,12,128]{3,1,2,0:T(8,128)(2,1)}, bf16[4,128,12,128]{3,1,2,0:T(8,128)(2,1)}, u32[]{:S(2)}, u32[]{:S(2)}) collective-permute-start(bf16[4,128,12,128]{3,1,2,0:T(8,128)(2,1)} %pad_maximum_fusion.1), channel_id=1, source_target_pairs={{0,16},{2,18},{4,20},{6,22},{8,24},{10,26},{12,28},{14,30},{1,17},... | collective-permute-start | bytes 4718600 | tf_op jit(solution)/shard_map/ppermute | solution.py:15
  285.2 328.9 %collective-permute-start.19 = (bf16[4,128,12,128]{3,1,2,0:T(8,128)(2,1)S(1)}, bf16[4,128,12,128]{3,1,2,0:T(8,128)(2,1)}, u32[]{:S(2)}, u32[]{:S(2)}) collective-permute-start(bf16[4,128,12,128]{3,1,2,0:T(8,128)(2,1)S(1)} %copy.204), channel_id=1, source_target_pairs={{16,0},{18,2},{20,4},{22,6},{24,8},{26,10},{28,12},{30,14},{17,1},... | collective-permute-start | bytes 4718600 | tf_op jit(solution)/shard_map/ppermute | solution.py:15
  319.0 167.6 %collective-permute-start.15 = (bf16[4,128,12,128]{3,1,2,0:T(8,128)(2,1)S(1)}, bf16[4,128,12,128]{3,1,2,0:T(8,128)(2,1)}, u32[]{:S(2)}, u32[]{:S(2)}) collective-permute-start(bf16[4,128,12,128]{3,1,2,0:T(8,128)(2,1)S(1)} %copy.204), channel_id=1, source_target_pairs={{8,0},{10,2},{12,4},{14,6},{16,8},{18,10},{20,12},{22,14},{24,16},... | collective-permute-start | bytes 4718600 | tf_op jit(solution)/shard_map/ppermute | solution.py:15
  329.9 140.7 %collective-permute-start.18 = (bf16[4,128,12,128]{3,1,2,0:T(8,128)(2,1)}, bf16[4,128,12,128]{3,1,2,0:T(8,128)(2,1)}, u32[]{:S(2)}, u32[]{:S(2)}) collective-permute-start(bf16[4,128,12,128]{3,1,2,0:T(8,128)(2,1)} %pad_maximum_fusion.1), channel_id=1, source_target_pairs={{16,0},{18,2},{20,4},{22,6},{24,8},{26,10},{28,12},{30,14},{17,1},... | collective-permute-start | bytes 4718600 | tf_op jit(solution)/shard_map/ppermute | solution.py:15
  335.8 5.9 copy-start.70
  335.8 89.8 %collective-permute-start.14 = (bf16[4,128,12,128]{3,1,2,0:T(8,128)(2,1)}, bf16[4,128,12,128]{3,1,2,0:T(8,128)(2,1)}, u32[]{:S(2)}, u32[]{:S(2)}) collective-permute-start(bf16[4,128,12,128]{3,1,2,0:T(8,128)(2,1)} %pad_maximum_fusion.1), channel_id=1, source_target_pairs={{8,0},{10,2},{12,4},{14,6},{16,8},{18,10},{20,12},{22,14},{24,16},... | collective-permute-start | bytes 4718600 | tf_op jit(solution)/shard_map/ppermute | solution.py:15
  341.7 4.4 copy-start.68
  355.0 6.1 copy-start.62
  355.0 89.0 %collective-permute-start.2 = (bf16[4,128,12,128]{3,1,2,0:T(8,128)(2,1)}, bf16[4,128,12,128]{3,1,2,0:T(8,128)(2,1)}, u32[]{:S(2)}, u32[]{:S(2)}) collective-permute-start(bf16[4,128,12,128]{3,1,2,0:T(8,128)(2,1)} %pad_maximum_fusion.1), channel_id=1, source_target_pairs={{2,0},{4,2},{6,4},{8,6},{10,8},{12,10},{14,12},{16,14},{18,16},{20... | collective-permute-start | bytes 4718600 | tf_op jit(solution)/shard_map/ppermute | solution.py:15
  361.0 4.4 copy-start.6
  361.0 4.4 copy-start.30
  373.5 57.9 %copy-start.60 = (pred[4]{0:T(512)(128)(4,1)S(1)}, pred[4]{0:T(512)(128)(4,1)}, u32[]{:S(2)}) copy-start(pred[4]{0:T(512)(128)(4,1)} %get-tuple-element.57) | copy-start | bytes 16
  425.7 27.6 %collective-permute-start = (bf16[4,128,12,128]{3,1,2,0:T(8,128)(2,1)}, bf16[4,128,12,128]{3,1,2,0:T(8,128)(2,1)}, u32[]{:S(2)}, u32[]{:S(2)}) collective-permute-start(bf16[4,128,12,128]{3,1,2,0:T(8,128)(2,1)} %pad_maximum_fusion.1), channel_id=1, source_target_pairs={{0,2},{2,4},{4,6},{6,8},{8,10},{10,12},{12,14},{14,16},{16,18},{18... | collective-permute-start | bytes 4718600 | tf_op jit(solution)/shard_map/ppermute | solution.py:15
  431.4 4.4 copy-start.12
  431.4 4.4 copy-start.27
  444.0 137.6 %collective-permute-start.17 = (bf16[4,128,12,128]{3,1,2,0:T(8,128)(2,1)S(1)}, bf16[4,128,12,128]{3,1,2,0:T(8,128)(2,1)}, u32[]{:S(2)}, u32[]{:S(2)}) collective-permute-start(bf16[4,128,12,128]{3,1,2,0:T(8,128)(2,1)S(1)} %copy.204), channel_id=1, source_target_pairs={{0,16},{2,18},{4,20},{6,22},{8,24},{10,26},{12,28},{14,30},{1,17},... | collective-permute-start | bytes 4718600 | tf_op jit(solution)/shard_map/ppermute | solution.py:15
  453.2 142.0 %collective-permute-start.3 = (bf16[4,128,12,128]{3,1,2,0:T(8,128)(2,1)S(1)}, bf16[4,128,12,128]{3,1,2,0:T(8,128)(2,1)}, u32[]{:S(2)}, u32[]{:S(2)}) collective-permute-start(bf16[4,128,12,128]{3,1,2,0:T(8,128)(2,1)S(1)} %copy.204), channel_id=1, source_target_pairs={{2,0},{4,2},{6,4},{8,6},{10,8},{12,10},{14,12},{16,14},{18,16},{20... | collective-permute-start | bytes 4718600 | tf_op jit(solution)/shard_map/ppermute | solution.py:15
  470.6 128.7 %collective-permute-start.1 = (bf16[4,128,12,128]{3,1,2,0:T(8,128)(2,1)S(1)}, bf16[4,128,12,128]{3,1,2,0:T(8,128)(2,1)}, u32[]{:S(2)}, u32[]{:S(2)}) collective-permute-start(bf16[4,128,12,128]{3,1,2,0:T(8,128)(2,1)S(1)} %copy.204), channel_id=1, source_target_pairs={{0,2},{2,4},{4,6},{6,8},{8,10},{10,12},{12,14},{14,16},{16,18},{18... | collective-permute-start | bytes 4718600 | tf_op jit(solution)/shard_map/ppermute | solution.py:15
  476.0 5.2 copy-start
  489.0 4.4 copy-start.7
  583.9 5.2 copy-start.5
  584.0 5.2 copy-start.14
  584.0 5.2 copy-start.61
  584.0 5.2 copy-start.63
  603.4 7.2 %copy-start.1 = (f32[4,12,128,256]{2,3,1,0:S(1)}, f32[4,12,128,256]{2,3,1,0}, u32[]{:S(2)}) copy-start(f32[4,12,128,256]{2,3,1,0} %get-tuple-element.84) | copy-start | bytes 18874372
  603.4 7.2 %copy-start.25 = (bf16[8,128,12,128]{3,1,2,0:T(8,128)(2,1)S(1)}, bf16[8,128,12,128]{3,1,2,0:T(8,128)(2,1)}, u32[]{:S(2)}) copy-start(bf16[8,128,12,128]{3,1,2,0:T(8,128)(2,1)} %gather_fusion.5) | copy-start | bytes 9437188
  (52 other events, 158.9 us)
where the time goes:
time: 662 us; the launch traced here: 655 us
  waiting for transfers between devices  256 us (39%)
  local copies, waits for them, and re-layouts  169 us (26%)
  matrix products  92.9 us (14%)
  starting transfers between devices  72.6 us (11%)
  other arithmetic  40.5 us (6%)
  blocking collectives  22.8 us (3%)
    ppermute x20, waiting for transfers between devices, from_behind(): return lax.ppermute(block, axis, route)  227 us
    ppermute x20, starting transfers between devices, from_behind(): return lax.ppermute(block, axis, route)  60.6 us
    dot_general x11, matrix products, frame_partial(): jnp.einsum('bhqsk,bskhd->bqhd', probs.astype(jnp.bfloat16), picked_values...  52 us
    gather x14, local copies, waits for them, and re-layouts, frame_partial(): picked_keys = key_blocks[block_ids]  51.4 us
    gather x11, local copies, waits for them, and re-layouts, frame_partial(): picked_values = value_blocks[block_ids]  37.4 us
    dot_general x8, matrix products, frame_partial(): jnp.einsum('bqhd,bskhd->bhqsk', query_group, picked_keys, preferred_eleme...  27.8 us
    reduce_sum x7, other arithmetic, frame_partial(): part_sum = jnp.sum(probs, axis=(3, 4))  23.8 us
    all_to_all x1, blocking collectives, local(): lax.all_to_all(attended, 'head', split_axis=0, concat_axis=1, tiled=True)  22.8 us
  transfers between devices with their start and end apart: 23, of which 8 were waited for; matrix products, arithmetic and copies ran while one was open for 43% of the time, Pallas kernels for 0%

commit v1 on v0

--- a/solution.py
+++ b/solution.py
@@ -7,6 +7,13 @@
 BLK = 128
 SLOTS = 4
 NEG_FILL = -1e30
+
+
+def stacked_exchange(x, name, split, join):
+    size = lax.axis_size(name)
+    blocks = jnp.stack(jnp.split(x, size, axis=split), axis=0)
+    blocks = lax.all_to_all(blocks, name, split_axis=0, concat_axis=0)
+    return jnp.concatenate(blocks, axis=join)
 
 
 def from_behind(block, axis, distance):
@@ -162,7 +169,7 @@
         state = merge_state(state, part)
     denominator = jnp.transpose(state[1], (0, 2, 1))[..., None]
     attended = (state[2] / denominator).reshape(frame_tokens, row_width).astype(jnp.bfloat16)
-    return lax.all_to_all(attended, "head", split_axis=0, concat_axis=1, tiled=True)
+    return stacked_exchange(attended, "head", 0, 1)
 
 
 def solution(mesh):

time: 662 us -> 663 us (level)
  no operation moved by 1% of the time
where the time goes in v1:
time: 663 us; the launch traced here: 655 us
  waiting for transfers between devices  256 us (39%)
  local copies, waits for them, and re-layouts  169 us (25%)
  matrix products  92.9 us (14%)
  starting transfers between devices  72.6 us (11%)
  other arithmetic  40.7 us (6%)
  blocking collectives  22.7 us (3%)
    ppermute x20, waiting for transfers between devices, from_behind(): return lax.ppermute(block, axis, route)  227 us
    ppermute x20, starting transfers between devices, from_behind(): return lax.ppermute(block, axis, route)  60.6 us
    dot_general x11, matrix products, frame_partial(): jnp.einsum('bhqsk,bskhd->bqhd', probs.astype(jnp.bfloat16), picked_values...  52 us
    gather x14, local copies, waits for them, and re-layouts, frame_partial(): picked_keys = key_blocks[block_ids]  51.4 us
    gather x11, local copies, waits for them, and re-layouts, frame_partial(): picked_values = value_blocks[block_ids]  37.4 us
    dot_general x8, matrix products, frame_partial(): jnp.einsum('bqhd,bskhd->bhqsk', query_group, picked_keys, preferred_eleme...  27.8 us
    reduce_sum x7, other arithmetic, frame_partial(): part_sum = jnp.sum(probs, axis=(3, 4))  23.8 us
    all_to_all x1, blocking collectives, stacked_exchange(): blocks = lax.all_to_all(blocks, name, split_axis=0, concat_axis=0)  22.7 us
  transfers between devices with their start and end apart: 23, of which 8 were waited for; matrix products, arithmetic and copies ran while one was open for 43% of the time, Pallas kernels for 0%

profile of v1, /device:TPU:26, one launch (start us, length us, event | category | flops | bytes accessed | tf_op | source)
XLA Modules:
  0.0 655.3 jit_solution(5578897673872795329)
XLA Ops:
  2.7 3.7 all-to-all-start.1
  9.6 16.3 %all-to-all-done.1 = bf16[256,2,1536]{0,2,1:T(8,128)(2,1)S(1)} async-done(((bf16[256,2,1536]{0,2,1:T(8,128)(2,1)}), bf16[256,2,1536]{0,2,1:T(8,128)(2,1)S(1)}, u32[]{:S(2)}, u32[]{:S(2)}) %all-to-all-start.1) | async-done | bytes 1572896 | tf_op jit(solution)/shard_map/all_to_all | solution.py:131
  25.9 3.7 all-to-all-start.2
  35.6 12.6 %all-to-all-done.2 = bf16[256,2,1536]{0,2,1:T(8,128)(2,1)S(1)} async-done(((bf16[256,2,1536]{0,2,1:T(8,128)(2,1)}), bf16[256,2,1536]{0,2,1:T(8,128)(2,1)S(1)}, u32[]{:S(2)}, u32[]{:S(2)}) %all-to-all-start.2) | async-done | bytes 1572896 | tf_op jit(solution)/shard_map/all_to_all | solution.py:132
  48.2 4.6 all-to-all-start
  54.6 10.7 %copy.205 = bf16[2,256,1536]{1,0,2:T(2,128)(2,1)} copy(bf16[2,256,1536]{1,2,0:T(8,128)(2,1)S(1)} %bitcast.450) | data formatting | bytes 3145728 | tf_op jit(solution)/shard_map/all_to_all | solution.py:132
  65.3 5.2 reshape.380
  79.4 10.7 %copy.197 = bf16[2,256,1536]{1,0,2:T(2,128)(2,1)} copy(bf16[2,256,1536]{1,2,0:T(8,128)(2,1)S(1)} %bitcast.449) | data formatting | bytes 3145728 | tf_op jit(solution)/shard_map/convert_element_type | solution.py:140
  94.1 4.8 copy.190
  106.9 3.7 concatenate.22
  115.3 3.7 copy.202
  120.6 4.0 pad_maximum_fusion.1
  125.8 6.1 collective-permute-start.10
  136.1 4.0 gather_fusion.1
  140.1 5.5 gather_fusion
  146.8 3.7 copy.195
  152.3 4.3 copy.203
  157.5 5.6 fusion
  163.2 5.7 collective-permute-start.7
  170.2 9.8 %collective-permute-done.12 = bf16[4,128,12,128]{3,1,2,0:T(8,128)(2,1)} collective-permute-done((bf16[4,128,12,128]{3,1,2,0:T(8,128)(2,1)}, bf16[4,128,12,128]{3,1,2,0:T(8,128)(2,1)}, u32[]{:S(2)}, u32[]{:S(2)}) %collective-permute-start.12) | collective-permute-done | bytes 1572896 | tf_op jit(solution)/shard_map/ppermute | solution.py:22
  183.7 11.9 %bitcast_convert_fusion.2 = bf16[4,12,128,128]{3,2,1,0:T(8,128)(2,1)} fusion(f32[4,12,128,512]{2,3,1,0} %get-tuple-element.90, f32[4,12,128]{2,1,0:T(8,128)S(1)} %get-tuple-element.89, pred[4,4]{1,0:T(4,128)(4,1)S(1)} %copy-done.73, bf16[4,4,128,12,128]{4,2,3,1,0:T(8,128)(2,1)} %bitcast.448), kind=kOutput, calls=%fused_computation.84 | convolution fusion | flops 821821440 | bytes 20471824 | tf_op jit(solution)/shard_map/bhqsk,bskhd->bqhd/dot_general | solution.py:99
  195.5 12.1 %collective-permute-done.8 = bf16[4,128,12,128]{3,1,2,0:T(8,128)(2,1)} collective-permute-done((bf16[4,128,12,128]{3,1,2,0:T(8,128)(2,1)}, bf16[4,128,12,128]{3,1,2,0:T(8,128)(2,1)}, u32[]{:S(2)}, u32[]{:S(2)}) %collective-permute-start.8) | collective-permute-done | bytes 1572896 | tf_op jit(solution)/shard_map/ppermute | solution.py:22
  209.2 6.6 %fusion.1 = f32[4,12,128]{2,1,0:T(8,128)S(1)} fusion(f32[4,12,128,512]{2,3,1,0} %get-tuple-element.90, f32[4,12,128]{2,1,0:T(8,128)S(1)} %get-tuple-element.89, pred[4,4]{1,0:T(4,128)(4,1)S(1)} %copy-done.73), kind=kLoop, calls=%fused_computation.25 | loop fusion | flops 15722496 | bytes 12632080 | tf_op jit(solution)/shard_map/reduce_sum | solution.py:98
  236.3 48.9 %collective-permute-done.7 = bf16[4,128,12,128]{3,1,2,0:T(8,128)(2,1)} collective-permute-done((bf16[4,128,12,128]{3,1,2,0:T(8,128)(2,1)S(1)}, bf16[4,128,12,128]{3,1,2,0:T(8,128)(2,1)}, u32[]{:S(2)}, u32[]{:S(2)}) %collective-permute-start.7) | collective-permute-done | bytes 1572896 | tf_op jit(solution)/shard_map/ppermute | solution.py:22
  285.3 9.1 %collective-permute-start.19 = (bf16[4,128,12,128]{3,1,2,0:T(8,128)(2,1)S(1)}, bf16[4,128,12,128]{3,1,2,0:T(8,128)(2,1)}, u32[]{:S(2)}, u32[]{:S(2)}) collective-permute-start(bf16[4,128,12,128]{3,1,2,0:T(8,128)(2,1)S(1)} %copy.206), channel_id=1, source_target_pairs={{16,0},{18,2},{20,4},{22,6},{24,8},{26,10},{28,12},{30,14},{17,1},... | collective-permute-start | bytes 4718600 | tf_op jit(solution)/shard_map/ppermute | solution.py:22
  297.7 21.3 %collective-permute-done.6 = bf16[4,128,12,128]{3,1,2,0:T(8,128)(2,1)} collective-permute-done((bf16[4,128,12,128]{3,1,2,0:T(8,128)(2,1)}, bf16[4,128,12,128]{3,1,2,0:T(8,128)(2,1)}, u32[]{:S(2)}, u32[]{:S(2)}) %collective-permute-start.6) | collective-permute-done | bytes 1572896 | tf_op jit(solution)/shard_map/ppermute | solution.py:22
  319.1 7.5 %collective-permute-start.15 = (bf16[4,128,12,128]{3,1,2,0:T(8,128)(2,1)S(1)}, bf16[4,128,12,128]{3,1,2,0:T(8,128)(2,1)}, u32[]{:S(2)}, u32[]{:S(2)}) collective-permute-start(bf16[4,128,12,128]{3,1,2,0:T(8,128)(2,1)S(1)} %copy.206), channel_id=1, source_target_pairs={{8,0},{10,2},{12,4},{14,6},{16,8},{18,10},{20,12},{22,14},{24,16},... | collective-permute-start | bytes 4718600 | tf_op jit(solution)/shard_map/ppermute | solution.py:22
  338.4 3.5 gather_fusion.6
  341.8 4.4 fusion.56
  361.2 4.4 fusion.60
  373.7 52.1 %collective-permute-done.14 = bf16[4,128,12,128]{3,1,2,0:T(8,128)(2,1)} collective-permute-done((bf16[4,128,12,128]{3,1,2,0:T(8,128)(2,1)}, bf16[4,128,12,128]{3,1,2,0:T(8,128)(2,1)}, u32[]{:S(2)}, u32[]{:S(2)}) %collective-permute-start.14) | collective-permute-done | bytes 1572896 | tf_op jit(solution)/shard_map/ppermute | solution.py:22
  431.5 4.4 fusion.61
  445.3 4.0 gather_fusion.4
  449.3 4.0 copy.213
  453.3 3.6 collective-permute-start.3
  457.0 4.0 gather_fusion.2
  463.3 3.7 fusion.11
  467.0 3.7 fusion.12
  476.1 5.2 fusion.13
  489.1 4.3 convolution_convert_fusion.2
  499.0 82.7 %collective-permute-done.17 = bf16[4,128,12,128]{3,1,2,0:T(8,128)(2,1)} collective-permute-done((bf16[4,128,12,128]{3,1,2,0:T(8,128)(2,1)S(1)}, bf16[4,128,12,128]{3,1,2,0:T(8,128)(2,1)}, u32[]{:S(2)}, u32[]{:S(2)}) %collective-permute-start.17) | collective-permute-done | bytes 1572896 | tf_op jit(solution)/shard_map/ppermute | solution.py:22
  584.1 4.3 convolution_convert_fusion.1
  595.4 4.0 gather_fusion.5
  599.4 4.1 gather_fusion.3
  603.5 7.2 %bitcast_convert_fusion.1 = bf16[4,12,128,128]{3,2,1,0:T(8,128)(2,1)} fusion(f32[4,12,128,256]{2,3,1,0} %get-tuple-element.88, f32[4,12,128]{2,1,0:T(8,128)S(1)} %get-tuple-element.87, pred[4,2]{1,0:T(4,128)(4,1)S(1)} %copy-done.54, bf16[4,2,128,12,128]{4,2,3,1,0:T(8,128)(2,1)} %bitcast.455), kind=kOutput, calls=%fused_computation.79 | convolution fusion | flops 411303936 | bytes 11034632 | tf_op jit(solution)/shard_map/bhqsk,bskhd->bqhd/dot_general | solution.py:99
  614.2 3.5 gather_fusion.21
  617.8 9.7 %fusion.23 = bf16[4,128,12,128]{1,3,2,0:T(8,128)(2,1)S(1)} fusion(bf16[4,12,128,128]{3,2,1,0:T(8,128)(2,1)} %convolution_convert_fusion.1, bf16[4,12,128,128]{3,2,1,0:T(8,128)(2,1)} %convolution_convert_fusion.2, bf16[4,12,128,128]{3,2,1,0:T(8,128)(2,1)} %convolution_convert_fusion.3, bf16[4,12,128,128]{3,2,1,0:T(8,128)(2,1)} %convolution_convert_fusion.4, ...), kind=kOutput, calls=%fused_computation.49 | convolution fusion | flops 241434624 | bytes 22609924 | tf_op jit(solution)/shard_map/bhqsk,bskhd->bqhd/dot_general | solution.py:99
  630.4 22.7 %all_to_all.47 = bf16[2,256,1536]{1,2,0:T(8,128)(2,1)S(1)} all-to-all(bf16[2,256,1536]{1,2,0:T(8,128)(2,1)S(1)} %pad_maximum_fusion.2), channel_id=1, replica_groups=mesh['seq'=16,'head'=2] {'head'}, dimensions={0} | all-to-all | bytes 3145728 | tf_op jit(solution)/shard_map/all_to_all | solution.py:15
  (287 shorter events, 168.8 us)
Async XLA Ops:
  0.0 6.5 copy-start.51
  0.0 7.4 %copy-start.31 = (bf16[256,3072]{1,0:T(8,128)(2,1)S(1)}, bf16[256,3072]{1,0:T(8,128)(2,1)}, u32[]{:S(2)}) copy-start(bf16[256,3072]{1,0:T(8,128)(2,1)} %param.7) | copy-start | bytes 4718596
  2.7 23.2 %all-to-all-start.1 = ((bf16[256,2,1536]{0,2,1:T(8,128)(2,1)}), bf16[256,2,1536]{0,2,1:T(8,128)(2,1)S(1)}, u32[]{:S(2)}, u32[]{:S(2)}) async-start(bf16[256,2,1536]{0,2,1:T(8,128)(2,1)} %bitcast.3), calls=%async_computation.1 | async-start | bytes 3145728 | tf_op jit(solution)/shard_map/all_to_all | solution.py:131
  25.9 22.3 %all-to-all-start.2 = ((bf16[256,2,1536]{0,2,1:T(8,128)(2,1)}), bf16[256,2,1536]{0,2,1:T(8,128)(2,1)S(1)}, u32[]{:S(2)}, u32[]{:S(2)}) async-start(bf16[256,2,1536]{0,2,1:T(8,128)(2,1)} %bitcast.451), calls=%async_computation.2 | async-start | bytes 3145728 | tf_op jit(solution)/shard_map/all_to_all | solution.py:132
  48.2 46.0 %all-to-all-start = ((bf16[256,2,1536]{0,2,1:T(8,128)(2,1)}), bf16[256,2,1536]{0,2,1:T(8,128)(2,1)}, u32[]{:S(2)}, u32[]{:S(2)}) async-start(bf16[256,2,1536]{0,2,1:T(8,128)(2,1)} %bitcast.452), calls=%async_computation | async-start | bytes 3145728 | tf_op jit(solution)/shard_map/all_to_all | solution.py:129
  73.2 61.4 %collective-permute-start.13 = (bf16[4,128,12,128]{3,1,2,0:T(8,128)(2,1)S(1)}, bf16[4,128,12,128]{3,1,2,0:T(8,128)(2,1)}, u32[]{:S(2)}, u32[]{:S(2)}) collective-permute-start(bf16[4,128,12,128]{3,1,2,0:T(8,128)(2,1)S(1)} %copy.206), channel_id=1, source_target_pairs={{0,8},{2,10},{4,12},{6,14},{8,16},{10,18},{12,20},{14,22},{16,24},... | collective-permute-start | bytes 4718600 | tf_op jit(solution)/shard_map/ppermute | solution.py:22
  74.5 88.7 %collective-permute-start.11 = (bf16[4,128,12,128]{3,1,2,0:T(8,128)(2,1)S(1)}, bf16[4,128,12,128]{3,1,2,0:T(8,128)(2,1)}, u32[]{:S(2)}, u32[]{:S(2)}) collective-permute-start(bf16[4,128,12,128]{3,1,2,0:T(8,128)(2,1)S(1)} %copy.206), channel_id=1, source_target_pairs={{6,0},{8,2},{10,4},{12,6},{14,8},{16,10},{18,12},{20,14},{22,16},{... | collective-permute-start | bytes 4718600 | tf_op jit(solution)/shard_map/ppermute | solution.py:22
  77.6 91.3 %collective-permute-start.9 = (bf16[4,128,12,128]{3,1,2,0:T(8,128)(2,1)S(1)}, bf16[4,128,12,128]{3,1,2,0:T(8,128)(2,1)}, u32[]{:S(2)}, u32[]{:S(2)}) collective-permute-start(bf16[4,128,12,128]{3,1,2,0:T(8,128)(2,1)S(1)} %copy.206), channel_id=1, source_target_pairs={{0,6},{2,8},{4,10},{6,12},{8,14},{10,16},{12,18},{14,20},{16,22},{... | collective-permute-start | bytes 4718600 | tf_op jit(solution)/shard_map/ppermute | solution.py:22
  101.7 34.4 %copy-start.22 = (bf16[512,12,128]{0,2,1:T(8,128)(2,1)}, bf16[512,12,128]{0,2,1:T(8,128)(2,1)S(1)}, u32[]{:S(2)}) copy-start(bf16[512,12,128]{0,2,1:T(8,128)(2,1)S(1)} %convert_element_type.181) | copy-start | bytes 4718596
  119.0 13.6 %copy-start.74 = (s32[4,1]{0,1:T(1,128)S(1)}, s32[4,1]{0,1:T(1,128)}, u32[]{:S(2)}) copy-start(s32[4,1]{0,1:T(1,128)} %copy.291) | copy-start | bytes 52
  119.0 17.0 %copy-start.32 = (bf16[512,12,8,1]{0,2,3,1:T(8,128)(2,1)S(1)}, bf16[512,12,8,1]{0,2,3,1:T(8,128)(2,1)}, u32[]{:S(2)}) copy-start(bf16[512,12,8,1]{0,2,3,1:T(8,128)(2,1)} %get-tuple-element.69) | copy-start | bytes 294916
  119.0 17.0 %copy-start.33 = (bf16[512,12,8,1]{0,2,3,1:T(8,128)(2,1)S(1)}, bf16[512,12,8,1]{0,2,3,1:T(8,128)(2,1)}, u32[]{:S(2)}) copy-start(bf16[512,12,8,1]{0,2,3,1:T(8,128)(2,1)} %get-tuple-element.70) | copy-start | bytes 294916
  120.6 11.3 %copy-start.72 = (s32[64,16]{0,1:T(8,128)S(1)}, s32[64,16]{0,1:T(8,128)}, u32[]{:S(2)}) copy-start(s32[64,16]{0,1:T(8,128)} %param.9) | copy-start | bytes 12292
  120.6 11.4 %copy-start.75 = (s32[4,1]{0,1:T(1,128)S(1)}, s32[4,1]{0,1:T(1,128)}, u32[]{:S(2)}) copy-start(s32[4,1]{0,1:T(1,128)} %copy.290) | copy-start | bytes 52
  124.5 55.4 %collective-permute-start.12 = (bf16[4,128,12,128]{3,1,2,0:T(8,128)(2,1)}, bf16[4,128,12,128]{3,1,2,0:T(8,128)(2,1)}, u32[]{:S(2)}, u32[]{:S(2)}) collective-permute-start(bf16[4,128,12,128]{3,1,2,0:T(8,128)(2,1)} %pad_maximum_fusion.1), channel_id=1, source_target_pairs={{0,8},{2,10},{4,12},{6,14},{8,16},{10,18},{12,20},{14,22},{16,24},... | collective-permute-start | bytes 4718600 | tf_op jit(solution)/shard_map/ppermute | solution.py:22
  125.8 56.6 %collective-permute-start.10 = (bf16[4,128,12,128]{3,1,2,0:T(8,128)(2,1)}, bf16[4,128,12,128]{3,1,2,0:T(8,128)(2,1)}, u32[]{:S(2)}, u32[]{:S(2)}) collective-permute-start(bf16[4,128,12,128]{3,1,2,0:T(8,128)(2,1)} %pad_maximum_fusion.1), channel_id=1, source_target_pairs={{6,0},{8,2},{10,4},{12,6},{14,8},{16,10},{18,12},{20,14},{22,16},{... | collective-permute-start | bytes 4718600 | tf_op jit(solution)/shard_map/ppermute | solution.py:22
  134.6 73.1 %collective-permute-start.8 = (bf16[4,128,12,128]{3,1,2,0:T(8,128)(2,1)}, bf16[4,128,12,128]{3,1,2,0:T(8,128)(2,1)}, u32[]{:S(2)}, u32[]{:S(2)}) collective-permute-start(bf16[4,128,12,128]{3,1,2,0:T(8,128)(2,1)} %pad_maximum_fusion.1), channel_id=1, source_target_pairs={{0,6},{2,8},{4,10},{6,12},{8,14},{10,16},{12,18},{14,20},{16,22},{... | collective-permute-start | bytes 4718600 | tf_op jit(solution)/shard_map/ppermute | solution.py:22
  140.1 5.5 slice-start
  163.2 122.1 %collective-permute-start.7 = (bf16[4,128,12,128]{3,1,2,0:T(8,128)(2,1)S(1)}, bf16[4,128,12,128]{3,1,2,0:T(8,128)(2,1)}, u32[]{:S(2)}, u32[]{:S(2)}) collective-permute-start(bf16[4,128,12,128]{3,1,2,0:T(8,128)(2,1)S(1)} %copy.206), channel_id=1, source_target_pairs={{4,0},{6,2},{8,4},{10,6},{12,8},{14,10},{16,12},{18,14},{20,16},{2... | collective-permute-start | bytes 4718600 | tf_op jit(solution)/shard_map/ppermute | solution.py:22
  168.9 161.1 %collective-permute-start.5 = (bf16[4,128,12,128]{3,1,2,0:T(8,128)(2,1)S(1)}, bf16[4,128,12,128]{3,1,2,0:T(8,128)(2,1)}, u32[]{:S(2)}, u32[]{:S(2)}) collective-permute-start(bf16[4,128,12,128]{3,1,2,0:T(8,128)(2,1)S(1)} %copy.206), channel_id=1, source_target_pairs={{0,4},{2,6},{4,8},{6,10},{8,12},{10,14},{12,16},{14,18},{16,20},{1... | collective-permute-start | bytes 4718600 | tf_op jit(solution)/shard_map/ppermute | solution.py:22
  180.0 139.1 %collective-permute-start.6 = (bf16[4,128,12,128]{3,1,2,0:T(8,128)(2,1)}, bf16[4,128,12,128]{3,1,2,0:T(8,128)(2,1)}, u32[]{:S(2)}, u32[]{:S(2)}) collective-permute-start(bf16[4,128,12,128]{3,1,2,0:T(8,128)(2,1)} %pad_maximum_fusion.1), channel_id=1, source_target_pairs={{4,0},{6,2},{8,4},{10,6},{12,8},{14,10},{16,12},{18,14},{20,16},{2... | collective-permute-start | bytes 4718600 | tf_op jit(solution)/shard_map/ppermute | solution.py:22
  182.4 153.5 %collective-permute-start.4 = (bf16[4,128,12,128]{3,1,2,0:T(8,128)(2,1)}, bf16[4,128,12,128]{3,1,2,0:T(8,128)(2,1)}, u32[]{:S(2)}, u32[]{:S(2)}) collective-permute-start(bf16[4,128,12,128]{3,1,2,0:T(8,128)(2,1)} %pad_maximum_fusion.1), channel_id=1, source_target_pairs={{0,4},{2,6},{4,8},{6,10},{8,12},{10,14},{12,16},{14,18},{16,20},{1... | collective-permute-start | bytes 4718600 | tf_op jit(solution)/shard_map/ppermute | solution.py:22
  207.7 147.4 %collective-permute-start.16 = (bf16[4,128,12,128]{3,1,2,0:T(8,128)(2,1)}, bf16[4,128,12,128]{3,1,2,0:T(8,128)(2,1)}, u32[]{:S(2)}, u32[]{:S(2)}) collective-permute-start(bf16[4,128,12,128]{3,1,2,0:T(8,128)(2,1)} %pad_maximum_fusion.1), channel_id=1, source_target_pairs={{0,16},{2,18},{4,20},{6,22},{8,24},{10,26},{12,28},{14,30},{1,17},... | collective-permute-start | bytes 4718600 | tf_op jit(solution)/shard_map/ppermute | solution.py:22
  285.3 328.9 %collective-permute-start.19 = (bf16[4,128,12,128]{3,1,2,0:T(8,128)(2,1)S(1)}, bf16[4,128,12,128]{3,1,2,0:T(8,128)(2,1)}, u32[]{:S(2)}, u32[]{:S(2)}) collective-permute-start(bf16[4,128,12,128]{3,1,2,0:T(8,128)(2,1)S(1)} %copy.206), channel_id=1, source_target_pairs={{16,0},{18,2},{20,4},{22,6},{24,8},{26,10},{28,12},{30,14},{17,1},... | collective-permute-start | bytes 4718600 | tf_op jit(solution)/shard_map/ppermute | solution.py:22
  319.1 167.6 %collective-permute-start.15 = (bf16[4,128,12,128]{3,1,2,0:T(8,128)(2,1)S(1)}, bf16[4,128,12,128]{3,1,2,0:T(8,128)(2,1)}, u32[]{:S(2)}, u32[]{:S(2)}) collective-permute-start(bf16[4,128,12,128]{3,1,2,0:T(8,128)(2,1)S(1)} %copy.206), channel_id=1, source_target_pairs={{8,0},{10,2},{12,4},{14,6},{16,8},{18,10},{20,12},{22,14},{24,16},... | collective-permute-start | bytes 4718600 | tf_op jit(solution)/shard_map/ppermute | solution.py:22
  330.0 140.7 %collective-permute-start.18 = (bf16[4,128,12,128]{3,1,2,0:T(8,128)(2,1)}, bf16[4,128,12,128]{3,1,2,0:T(8,128)(2,1)}, u32[]{:S(2)}, u32[]{:S(2)}) collective-permute-start(bf16[4,128,12,128]{3,1,2,0:T(8,128)(2,1)} %pad_maximum_fusion.1), channel_id=1, source_target_pairs={{16,0},{18,2},{20,4},{22,6},{24,8},{26,10},{28,12},{30,14},{17,1},... | collective-permute-start | bytes 4718600 | tf_op jit(solution)/shard_map/ppermute | solution.py:22
  335.9 5.9 copy-start.70
  335.9 89.8 %collective-permute-start.14 = (bf16[4,128,12,128]{3,1,2,0:T(8,128)(2,1)}, bf16[4,128,12,128]{3,1,2,0:T(8,128)(2,1)}, u32[]{:S(2)}, u32[]{:S(2)}) collective-permute-start(bf16[4,128,12,128]{3,1,2,0:T(8,128)(2,1)} %pad_maximum_fusion.1), channel_id=1, source_target_pairs={{8,0},{10,2},{12,4},{14,6},{16,8},{18,10},{20,12},{22,14},{24,16},... | collective-permute-start | bytes 4718600 | tf_op jit(solution)/shard_map/ppermute | solution.py:22
  341.8 4.4 copy-start.20
  341.8 4.4 copy-start.68
  355.1 6.1 copy-start.62
  355.1 88.9 %collective-permute-start.2 = (bf16[4,128,12,128]{3,1,2,0:T(8,128)(2,1)}, bf16[4,128,12,128]{3,1,2,0:T(8,128)(2,1)}, u32[]{:S(2)}, u32[]{:S(2)}) collective-permute-start(bf16[4,128,12,128]{3,1,2,0:T(8,128)(2,1)} %pad_maximum_fusion.1), channel_id=1, source_target_pairs={{2,0},{4,2},{6,4},{8,6},{10,8},{12,10},{14,12},{16,14},{18,16},{20... | collective-permute-start | bytes 4718600 | tf_op jit(solution)/shard_map/ppermute | solution.py:22
  361.2 4.4 copy-start.6
  361.2 4.4 copy-start.30
  373.7 57.8 %copy-start.60 = (pred[4]{0:T(512)(128)(4,1)S(1)}, pred[4]{0:T(512)(128)(4,1)}, u32[]{:S(2)}) copy-start(pred[4]{0:T(512)(128)(4,1)} %get-tuple-element.59) | copy-start | bytes 16
  425.7 27.6 %collective-permute-start = (bf16[4,128,12,128]{3,1,2,0:T(8,128)(2,1)}, bf16[4,128,12,128]{3,1,2,0:T(8,128)(2,1)}, u32[]{:S(2)}, u32[]{:S(2)}) collective-permute-start(bf16[4,128,12,128]{3,1,2,0:T(8,128)(2,1)} %pad_maximum_fusion.1), channel_id=1, source_target_pairs={{0,2},{2,4},{4,6},{6,8},{8,10},{10,12},{12,14},{14,16},{16,18},{18... | collective-permute-start | bytes 4718600 | tf_op jit(solution)/shard_map/ppermute | solution.py:22
  431.5 4.4 copy-start.12
  431.5 4.4 copy-start.27
  444.0 137.6 %collective-permute-start.17 = (bf16[4,128,12,128]{3,1,2,0:T(8,128)(2,1)S(1)}, bf16[4,128,12,128]{3,1,2,0:T(8,128)(2,1)}, u32[]{:S(2)}, u32[]{:S(2)}) collective-permute-start(bf16[4,128,12,128]{3,1,2,0:T(8,128)(2,1)S(1)} %copy.206), channel_id=1, source_target_pairs={{0,16},{2,18},{4,20},{6,22},{8,24},{10,26},{12,28},{14,30},{1,17},... | collective-permute-start | bytes 4718600 | tf_op jit(solution)/shard_map/ppermute | solution.py:22
  453.3 142.1 %collective-permute-start.3 = (bf16[4,128,12,128]{3,1,2,0:T(8,128)(2,1)S(1)}, bf16[4,128,12,128]{3,1,2,0:T(8,128)(2,1)}, u32[]{:S(2)}, u32[]{:S(2)}) collective-permute-start(bf16[4,128,12,128]{3,1,2,0:T(8,128)(2,1)S(1)} %copy.206), channel_id=1, source_target_pairs={{2,0},{4,2},{6,4},{8,6},{10,8},{12,10},{14,12},{16,14},{18,16},{20... | collective-permute-start | bytes 4718600 | tf_op jit(solution)/shard_map/ppermute | solution.py:22
  470.7 128.7 %collective-permute-start.1 = (bf16[4,128,12,128]{3,1,2,0:T(8,128)(2,1)S(1)}, bf16[4,128,12,128]{3,1,2,0:T(8,128)(2,1)}, u32[]{:S(2)}, u32[]{:S(2)}) collective-permute-start(bf16[4,128,12,128]{3,1,2,0:T(8,128)(2,1)S(1)} %copy.206), channel_id=1, source_target_pairs={{0,2},{2,4},{4,6},{6,8},{8,10},{10,12},{12,14},{14,16},{16,18},{18... | collective-permute-start | bytes 4718600 | tf_op jit(solution)/shard_map/ppermute | solution.py:22
  476.1 5.2 copy-start
  584.1 5.2 copy-start.5
  584.1 5.2 copy-start.14
  584.1 5.2 copy-start.61
  584.1 5.2 copy-start.63
  603.5 7.2 %copy-start.1 = (f32[4,12,128,256]{2,3,1,0:S(1)}, f32[4,12,128,256]{2,3,1,0}, u32[]{:S(2)}) copy-start(f32[4,12,128,256]{2,3,1,0} %get-tuple-element.86) | copy-start | bytes 18874372
  603.5 7.2 %copy-start.25 = (bf16[8,128,12,128]{3,1,2,0:T(8,128)(2,1)S(1)}, bf16[8,128,12,128]{3,1,2,0:T(8,128)(2,1)}, u32[]{:S(2)}) copy-start(bf16[8,128,12,128]{3,1,2,0:T(8,128)(2,1)} %gather_fusion.5) | copy-start | bytes 9437188
  (52 other events, 159.0 us)
